TPU v7x, 128 devices: a whole 4x4x4 slice. The times are simulated.
128 devices in a mesh: req: 32 (over x, y, z_hi), rep: 4 (over z_lo, core).
Axes of the slice: x: 4, y: 4, z: 4 (z_hi: 2, z_lo: 2; z = z_hi * 2 + z_lo), core: 2. Of those that a mesh axis runs over, the one named last changes fastest.
Arguments:
- tokens: bfloat16 [128, 2, 2048], P('req'), may hold values from -6 to 6
- norm_gains: float32 [2, 2048], replicated, may hold values from 0.1 to 1.9
- w_kv: bfloat16 [2048, 2, 2048], P(None, None, 'rep'), may hold values from -0.125 to 0.125
- w_query: bfloat16 [32, 2048, 512], P('req', None, 'rep'), may hold values from -0.125 to 0.125
- w_out: bfloat16 [32, 512, 2048], P('req', 'rep'), may hold values from -0.5 to 0.5
- w_gate: bfloat16 [32, 2048, 1408], P('req', None, 'rep'), may hold values from -0.125 to 0.125
- w_up: bfloat16 [32, 2048, 1408], P('req', None, 'rep'), may hold values from -0.125 to 0.125
- w_down: bfloat16 [32, 1408, 2048], P('req', 'rep'), may hold values from -0.078125 to 0.078125
- kv_pages: bfloat16 [8192, 16, 2, 2048], P('req', None, None, 'rep'), may hold values from -80 to 80
- page_table: int32 [128, 64], P('req'), may hold values from 0 to 255, as said below
- cache_len: int32 [128], P('req'), may hold values from 1 to 1024
- route_ids: int32 [128, 2, 2, 2], P('req'), may hold values from 0 to 7, all different within a row
- route_gates: bfloat16 [128, 2, 2, 2], P('req'), may hold values from 0.19921875 to 1
- new_slot: int32 [128], P('req'), may hold values from 0 to 127, each once
Outputs:
- layer_out: bfloat16 [128, 2, 2048], P('req')
Inputs may be any that keep to these rules, and one draw needn't show every extreme that they name: `page_table`: row i lists 64 distinct pages of the pool of the device that holds request i; two requests of one device share no page.
All inputs are finite; a program needn't handle non-finite values.
Results may differ from a plain program's by a relative error of at most 0.022.
Values may be sent and summed in bfloat16 or wider, within the bound.
No kernel may reach another device: no remote copies, remote signals or barrier semaphores. Data moves between devices by JAX's collectives and lax.ppermute only.
A program may use at most 128 MiB of HBM per device.

v0:
```python
import math
import jax
import jax.numpy as jnp
from jax import lax
from jax.sharding import PartitionSpec as P

HD = 128
EXPERTS = 8
EPSILON = 1e-06
MASKED = -1e30


def normalize(values, gain_row):
    scaling = lax.rsqrt(jnp.mean(values * values, axis=-1, keepdims=True) + EPSILON)
    return (values * scaling * gain_row).astype(jnp.bfloat16)


def expert_share(ids_block, gates_block, expert):
    return jnp.sum(jnp.where(ids_block == expert, gates_block.astype(jnp.float32), 0.0), axis=-1)


def attend(queries, cache_keys, cache_values, lengths, extra_keys, extra_values, extra_live):
    inv_scale = 1.0 / math.sqrt(queries.shape[-1])
    cache_scores = (
        jnp.einsum("jskhc,jlhc->jskhl", queries, cache_keys, preferred_element_type=jnp.float32)
        * inv_scale
    )
    alive_mask = jnp.arange(cache_keys.shape[1], dtype=jnp.int32)[None, :] < lengths[:, None]
    cache_scores = jnp.where(alive_mask[:, None, None, None, :], cache_scores, MASKED)
    extra_scores = (
        jnp.einsum("jskhc,jxhc->jskhx", queries, extra_keys, preferred_element_type=jnp.float32)
        * inv_scale
    )
    extra_scores = jnp.where(extra_live[None, :, None, None, :], extra_scores, MASKED)
    highest = jnp.maximum(jnp.max(cache_scores, axis=-1), jnp.max(extra_scores, axis=-1))[..., None]
    cache_exp = jnp.exp(cache_scores - highest)
    extra_exp = jnp.exp(extra_scores - highest)
    denominator = (jnp.sum(cache_exp, axis=-1) + jnp.sum(extra_exp, axis=-1))[..., None]
    cache_weight = (cache_exp / denominator).astype(jnp.bfloat16)
    extra_weight = (extra_exp / denominator).astype(jnp.bfloat16)
    mixture = jnp.einsum(
        "jskhl,jlhc->jskhc", cache_weight, cache_values, preferred_element_type=jnp.float32
    )
    mixture = mixture + jnp.einsum(
        "jskhx,jxhc->jskhc", extra_weight, extra_values, preferred_element_type=jnp.float32
    )
    return mixture.astype(jnp.bfloat16)


def combine(term_fn, all_rows):
    partial_value = lax.psum_scatter(
        term_fn(jnp.int32(0), all_rows // lax.axis_size("req") * lax.axis_size("req")).astype(
            jnp.bfloat16
        ),
        "req",
        scatter_dimension=0,
        tiled=True,
    )
    return lax.psum(partial_value, "rep").astype(jnp.float32)


def shards(
    tokens,
    norm_gains,
    w_kv,
    w_query,
    w_out,
    w_gate,
    w_up,
    w_down,
    kv_pages,
    page_table,
    cache_len,
    route_ids,
    route_gates,
    new_slot,
):
    rows_dev = tokens.shape[0]
    req_count = lax.axis_size("req")
    all_rows = rows_dev * req_count
    holders = req_count // EXPERTS
    expert = lax.axis_index("req") // holders
    head_dim = HD
    heads_rep = kv_pages.shape[-1] // head_dim
    heads_dev = w_query.shape[-1] // head_dim
    inputs = tokens.astype(jnp.float32)
    normed = normalize(inputs, norm_gains[0])
    cache_pages = kv_pages[page_table].reshape(rows_dev, -1, 2, heads_rep, head_dim)
    cache_keys = cache_pages[:, :, 0]
    cache_values = cache_pages[:, :, 1]
    experts_row = jnp.arange(EXPERTS, dtype=jnp.int32)

    def fresh_kv(normed_rows):
        return jnp.einsum(
            "jd,dtc->jtc", normed_rows, w_kv, preferred_element_type=jnp.float32
        ).astype(jnp.bfloat16)

    def pair_kv(first_kv, second_kv):
        return jnp.stack([first_kv, second_kv], axis=1).reshape(rows_dev, 2, 2, heads_rep, head_dim)

    first_fresh = fresh_kv(normed[:, 0])

    def section(step_list, gathered, slot_map, all_ids, all_gates, extra_kv):
        step_count = len(step_list)
        first_step = step_list[0]
        step_span = slice(first_step, first_step + step_count)
        inverse = (
            jnp.zeros((all_rows,), jnp.int32)
            .at[slot_map]
            .set(jnp.arange(all_rows, dtype=jnp.int32))
        )
        queries = jnp.einsum(
            "bsd,dc->bsc", gathered, w_query[0], preferred_element_type=jnp.float32
        ).astype(jnp.bfloat16)
        columns = []
        own_ids = []
        for position, current in enumerate(step_list):
            if current == 0:
                columns.append(queries[:, position])
                own_ids.append(route_ids[:, 0, 0])
            else:
                columns.append(jnp.take(queries[:, position], slot_map, axis=0))
                own_ids.append(jnp.take(all_ids[:, 0, 1], new_slot, axis=0))
        ordered = jnp.stack(columns, axis=1).reshape(
            req_count, rows_dev, step_count, heads_dev * head_dim
        )
        arrived = lax.all_to_all(ordered, "req", split_axis=0, concat_axis=0, tiled=True)
        arrived = arrived.reshape(EXPERTS, holders, rows_dev, step_count, heads_dev, head_dim)
        chosen = (jnp.stack(own_ids, axis=1)[..., None] == experts_row).astype(jnp.bfloat16)
        picked = jnp.einsum(
            "jske,egjshc->jskghc", chosen, arrived, preferred_element_type=jnp.float32
        ).astype(jnp.bfloat16)
        picked = picked.reshape(rows_dev, step_count, 2, heads_rep, head_dim)
        extra_live = jnp.array(
            [[extra_slot <= current for extra_slot in range(2)] for current in step_list]
        )
        result = attend(
            picked,
            cache_keys,
            cache_values,
            cache_len,
            extra_kv[:, :, 0],
            extra_kv[:, :, 1],
            extra_live,
        )
        result = result.reshape(rows_dev, step_count, 2, holders, heads_dev, head_dim)
        spread = jnp.einsum(
            "jske,jskghc->egjshc", chosen, result, preferred_element_type=jnp.float32
        ).astype(jnp.bfloat16)
        returned = lax.all_to_all(
            spread.reshape(req_count, rows_dev, step_count, heads_dev * head_dim),
            "req",
            split_axis=0,
            concat_axis=0,
            tiled=True,
        )
        returned = returned.reshape(all_rows, step_count, heads_dev * head_dim)
        answers = jnp.stack(
            [
                (
                    returned[:, position]
                    if current == 0
                    else jnp.take(returned[:, position], inverse, axis=0)
                )
                for position, current in enumerate(step_list)
            ],
            axis=1,
        )
        attn_share = expert_share(all_ids[:, 0, step_span], all_gates[:, 0, step_span], expert)
        ffn_share = expert_share(all_ids[:, 1, step_span], all_gates[:, 1, step_span], expert)

        def attn_term(first_row, row_count):
            return (
                jnp.einsum("bsc,cd->bsd", answers, w_out[0], preferred_element_type=jnp.float32)
                * attn_share[..., None]
            )

        hidden = inputs[:, step_span] + combine(attn_term, all_rows)
        hidden_normed = normalize(hidden, norm_gains[1])
        block_rows = lax.all_gather(hidden_normed, "req", axis=0, tiled=True)
        gate_part = jnp.einsum(
            "bsd,df->bsf", block_rows, w_gate[0], preferred_element_type=jnp.float32
        )
        up_part = jnp.einsum("bsd,df->bsf", block_rows, w_up[0], preferred_element_type=jnp.float32)
        hidden_units = (jax.nn.silu(gate_part) * up_part).astype(jnp.bfloat16)

        def ffn_term(first_row, row_count):
            return (
                jnp.einsum(
                    "bsf,fd->bsd", hidden_units, w_down[0], preferred_element_type=jnp.float32
                )
                * ffn_share[..., None]
            )

        return (hidden + combine(ffn_term, all_rows)).astype(jnp.bfloat16)

    first_rows, all_ids, all_gates, slot_map = (
        lax.all_gather(normed[:, 0:1], "req", axis=0, tiled=True),
        lax.all_gather(route_ids, "req", axis=0, tiled=True),
        lax.all_gather(route_gates, "req", axis=0, tiled=True),
        lax.all_gather(new_slot, "req", axis=0, tiled=True),
    )
    early = section(
        (0,), first_rows, slot_map, all_ids, all_gates, pair_kv(first_fresh, first_fresh)
    )
    second_rows = lax.all_gather(normed[:, 1:2], "req", axis=0, tiled=True)
    second_fresh = fresh_kv(jnp.take(second_rows[:, 0], new_slot, axis=0))
    later = section(
        (1,), second_rows, slot_map, all_ids, all_gates, pair_kv(first_fresh, second_fresh)
    )
    return jnp.concatenate([early, later], axis=1)


def solution(mesh):
    in_specs = (
        P("req", None, None),
        P(),
        P(None, None, "rep"),
        P("req", None, "rep"),
        P("req", "rep", None),
        P("req", None, "rep"),
        P("req", None, "rep"),
        P("req", "rep", None),
        P("req", None, None, "rep"),
        P("req", None),
        P("req"),
        P("req", None, None, None),
        P("req", None, None, None),
        P("req"),
    )
    out_specs = P("req", None, None)
    return jax.shard_map(shards, mesh=mesh, in_specs=in_specs, out_specs=out_specs, check_vma=False)
```

profile of v0, /device:TPU:1, one launch (start us, length us, event | category | flops | bytes accessed | tf_op | source)
XLA Modules:
  0.0 1477.4 jit_solution(3638717455090007884)
XLA Ops:
  6.5 1.0 multiply_reduce_fusion
  7.5 0.8 fusion.155
  8.3 0.8 multiply_convert_fusion
  9.2 88.1 %all_gather.21 = bf16[128,1,2048]{2,1,0:T(2,128)(2,1)S(1)} all-gather(bf16[4,1,2048]{2,1,0:T(2,128)(2,1)S(1)} %copy.217), channel_id=1, replica_groups=mesh['req'=32,'rep'=4] {'req'}, dimensions={0}, use_global_device_ids=true | all-gather | bytes 540672 | tf_op jit(solution)/shard_map/all_gather | solution.py:198
  97.3 2.1 convolution_convert_fusion.3
  99.4 3.9 all-to-all-start
  103.3 0.7 compare_and_fusion.2
  104.0 0.7 compare_select_fusion.3
  104.6 1.4 fusion.156
  106.7 0.9 dynamic-update-slice
  107.6 16.5 %all-reduce = s32[128]{0:T(128)S(1)} all-reduce(s32[128]{0:T(128)S(1)} %dynamic-update-slice), channel_id=1, replica_groups=mesh['req'=32,'rep'=4] {'req'}, use_global_device_ids=true, to_apply=%add | all-reduce | flops 128 | bytes 1024
  124.1 1.0 scatter_custom_fusion
  126.2 0.7 slice_bitcast_fusion
  126.9 0.8 copy.233
  127.7 0.7 compare_select_fusion
  128.5 0.7 iota_compare_fusion
  129.2 0.9 copy.235
  130.0 2.8 fusion.46
  132.9 76.8 %all_gather.23 = bf16[128,2,2,2]{3,2,1,0:T(2,128)(2,1)S(1)} all-gather(bf16[4,2,2,2]{3,2,1,0:T(2,128)(2,1)S(1)} %copy.235), channel_id=1, replica_groups=mesh['req'=32,'rep'=4] {'req'}, dimensions={0}, use_global_device_ids=true | all-gather | bytes 2112 | tf_op jit(solution)/shard_map/all_gather | solution.py:200
  209.7 0.8 fusion.153
  210.5 75.0 %all_gather.22 = s32[128,2,2,2]{3,2,1,0:T(2,128)S(1)} all-gather(s32[4,2,2,2]{3,2,1,0:T(2,128)S(1)} %copy.233), channel_id=1, replica_groups=mesh['req'=32,'rep'=4] {'req'}, dimensions={0}, use_global_device_ids=true | all-gather | bytes 4224 | tf_op jit(solution)/shard_map/all_gather | solution.py:199
  285.6 0.8 fusion.152
  286.4 82.6 %all_gather.25 = bf16[128,1,2048]{2,1,0:T(2,128)(2,1)S(1)} all-gather(bf16[4,1,2048]{2,1,0:T(2,128)(2,1)S(1)} %copy.241), channel_id=1, replica_groups=mesh['req'=32,'rep'=4] {'req'}, dimensions={0}, use_global_device_ids=true | all-gather | bytes 540672 | tf_op jit(solution)/shard_map/all_gather | solution.py:206
  370.8 2.9 fusion.49
  373.7 25.4 %gather_fusion = bf16[256,16,2,512]{3,2,1,0:T(2,128)(2,1)} fusion(bf16[256,16,2,512]{3,2,1,0:T(2,128)(2,1)} %param.26, s32[1024]{0:T(1024)S(1)} %pad_clamp_fusion.3), kind=kCustom, calls=%fused_computation.2 | custom fusion | bytes 16778240 | tf_op jit(solution)/shard_map/gather | solution.py:88
  399.1 14.0 reshape.554
  413.1 8.1 fusion.151
  421.2 0.7 gather_fusion.3
  421.9 0.7 broadcast_select_fusion
  422.6 0.7 select_reduce_fusion.1
  423.4 4.0 all-to-all-start.2
  427.8 8.1 all-to-all-done.2
  436.1 3.6 fusion.157
  439.7 1.3 fusion.158
  443.3 3.7 fusion.1
  447.1 1.4 fusion
  448.6 1.7 fusion.43
  450.3 0.8 copy.255
  451.7 3.9 all-to-all-start.3
  455.6 1.7 fusion.42
  457.2 0.8 copy.231
  458.0 0.6 copy.232
  458.7 5.5 all-to-all-done.3
  464.2 4.6 all-to-all-start.1
  469.4 1.3 gather_fusion.4
  470.7 6.6 all-to-all-done.1
  477.4 1.8 fusion.15
  479.2 1.9 fusion.13
  481.8 1.0 select_reduce_fusion
  482.9 388.7 %all-reduce.14.cloned.1.call-done = (bf16[128,1,2048]{2,0,1:T(8,128)(2,1)}, bf16[128,1,2048]{2,0,1:T(8,128)(2,1)}) async-done(((bf16[128,1,2048]{2,0,1:T(8,128)(2,1)}, bf16[128,1,2048]{2,0,1:T(8,128)(2,1)}), (bf16[128,1,2048]{2,0,1:T(8,128)(2,1)}, bf16[128,1,2048]{2,0,1:T(8,128)(2,1)})) %all-reduce.14.cloned.1.call-update) | async-done | bytes 1048592
  871.6 0.8 constant_dynamic-slice_fusion.3
  872.3 0.8 constant_dynamic-slice_fusion.1
  873.1 32.1 %all-reduce.8 = (bf16[4,1,2048]{2,0,1:T(4,128)(2,1)S(1)}, bf16[4,1,2048]{2,0,1:T(4,128)(2,1)S(1)}) all-reduce(bf16[4,1,2048]{2,0,1:T(4,128)(2,1)S(1)} %constant_dynamic-slice_fusion.3, bf16[4,1,2048]{2,0,1:T(4,128)(2,1)S(1)} %constant_dynamic-slice_fusion.1), channel_id=1, replica_groups=mesh['req'=32,'rep'=4] {'rep'}, use_global_device_ids=true, to_apply=%region_7.8 | all-reduce | flops 16384 | bytes 65536 | tf_op jit(solution)/shard_map/psum | solution.py:59
  905.5 87.1 %all_gather.27 = bf16[128,1,2048]{2,1,0:T(2,128)(2,1)S(1)} all-gather(bf16[4,1,2048]{2,1,0:T(2,128)(2,1)S(1)} %copy.258), channel_id=1, replica_groups=mesh['req'=32,'rep'=4] {'req'}, dimensions={0}, use_global_device_ids=true | all-gather | bytes 540672 | tf_op jit(solution)/shard_map/all_gather | solution.py:180
  992.7 79.9 %all_gather.24 = bf16[128,1,2048]{2,1,0:T(2,128)(2,1)S(1)} all-gather(bf16[4,1,2048]{2,1,0:T(2,128)(2,1)S(1)} %copy.237), channel_id=1, replica_groups=mesh['req'=32,'rep'=4] {'req'}, dimensions={0}, use_global_device_ids=true | all-gather | bytes 540672 | tf_op jit(solution)/shard_map/all_gather | solution.py:180
  1072.6 0.6 fusion.22
  1073.3 0.6 fusion.24
  1074.0 4.1 fusion.12
  1078.0 3.7 fusion.14
  1081.7 354.5 %all-reduce.12.cloned.1.call-done = (bf16[128,1,2048]{2,0,1:T(8,128)(2,1)}, bf16[128,1,2048]{2,0,1:T(8,128)(2,1)}) async-done(((bf16[128,1,2048]{2,0,1:T(8,128)(2,1)}, bf16[128,1,2048]{2,0,1:T(8,128)(2,1)}), (bf16[128,1,2048]{2,0,1:T(8,128)(2,1)}, bf16[128,1,2048]{2,0,1:T(8,128)(2,1)})) %all-reduce.12.cloned.1.call-update) | async-done | bytes 1048592
  1436.2 0.8 constant_dynamic-slice_fusion
  1437.0 0.8 constant_dynamic-slice_fusion.2
  1437.7 32.1 %all-reduce.7 = (bf16[4,1,2048]{2,0,1:T(4,128)(2,1)S(1)}, bf16[4,1,2048]{2,0,1:T(4,128)(2,1)S(1)}) all-reduce(bf16[4,1,2048]{2,0,1:T(4,128)(2,1)S(1)} %constant_dynamic-slice_fusion, bf16[4,1,2048]{2,0,1:T(4,128)(2,1)S(1)} %constant_dynamic-slice_fusion.2), channel_id=1, replica_groups=mesh['req'=32,'rep'=4] {'rep'}, use_global_device_ids=true, to_apply=%region_23.25 | all-reduce | flops 16384 | bytes 65536 | tf_op jit(solution)/shard_map/psum | solution.py:59
  1469.9 0.6 copy.261
  (98 shorter events, 7.9 us)
Async XLA Ops:
  6.5 1067.4 %copy-start = (bf16[1,352,2048]{2,1,0:T(8,128)(2,1)S(1)}, bf16[1,352,2048]{2,1,0:T(8,128)(2,1)}, u32[]{:S(2)}) copy-start(bf16[1,352,2048]{2,1,0:T(8,128)(2,1)} %param.25) | copy-start | bytes 4325380
  99.4 324.0 %all-to-all-start = ((bf16[32,4,1,128]{3,1,2,0:T(4,128)(2,1)}), bf16[32,4,1,128]{3,1,2,0:T(4,128)(2,1)S(1)}, u32[]{:S(2)}, u32[]{:S(2)}) async-start(bf16[32,4,1,128]{3,1,2,0:T(4,128)(2,1)} %bitcast.8), calls=%async_computation | async-start | bytes 65536 | tf_op jit(solution)/shard_map/all_to_all | solution.py:127
  129.2 240.1 %copy-start.8 = (bf16[1,2048,128]{2,1,0:T(8,128)(2,1)S(1)}, bf16[1,2048,128]{2,1,0:T(8,128)(2,1)}, u32[]{:S(2)}) copy-start(bf16[1,2048,128]{2,1,0:T(8,128)(2,1)} %param.21) | copy-start | bytes 1572868
  370.8 65.1 %copy-start.14 = (s32[4,2]{1,0:T(4,128)}, s32[4,2]{1,0:T(4,128)S(1)}, u32[]{:S(2)}) copy-start(s32[4,2]{1,0:T(4,128)S(1)} %broadcast_select_fusion.1) | copy-start | bytes 100
  423.4 16.4 %copy-start.13 = (s32[4,2]{1,0:T(4,128)}, s32[4,2]{1,0:T(4,128)S(1)}, u32[]{:S(2)}) copy-start(s32[4,2]{1,0:T(4,128)S(1)} %copy.216) | copy-start | bytes 100
  423.4 25.2 %copy-start.10 = (bf16[4,1,2,4,128]{4,1,3,0,2:T(2,128)(2,1)}, bf16[4,1,2,4,128]{4,1,3,0,2:T(2,128)(2,1)S(1)}, u32[]{:S(2)}) copy-start(bf16[4,1,2,4,128]{4,1,3,0,2:T(2,128)(2,1)S(1)} %stack.20) | copy-start | bytes 24580
  423.4 17.6 %copy-start.11 = (bf16[4,1,2,4,128]{4,1,3,0,2:T(2,128)(2,1)}, bf16[4,1,2,4,128]{4,1,3,0,2:T(2,128)(2,1)S(1)}, u32[]{:S(2)}) copy-start(bf16[4,1,2,4,128]{4,1,3,0,2:T(2,128)(2,1)S(1)} %stack.19) | copy-start | bytes 24580
  423.4 12.5 all-to-all-start.2
  435.9 3.8 copy-start.6
  439.7 2.1 copy-start.12
  443.3 3.7 copy-start.5
  447.1 1.5 copy-start.15
  447.1 30.3 %copy-start.7 = (bf16[1,128,2048]{2,1,0:T(8,128)(2,1)S(1)}, bf16[1,128,2048]{2,1,0:T(8,128)(2,1)}, u32[]{:S(2)}) copy-start(bf16[1,128,2048]{2,1,0:T(8,128)(2,1)} %param.22) | copy-start | bytes 1572868
  448.5 34.4 %copy-start.9 = (bf16[4,2,2048]{2,1,0:T(2,128)(2,1)S(1)}, bf16[4,2,2048]{2,1,0:T(2,128)(2,1)}, u32[]{:S(2)}) copy-start(bf16[4,2,2048]{2,1,0:T(2,128)(2,1)} %param.18) | copy-start | bytes 98308
  448.5 624.1 %copy-start.1 = (bf16[1,2048,352]{1,2,0:T(8,128)(2,1)S(1)}, bf16[1,2048,352]{1,2,0:T(8,128)(2,1)}, u32[]{:S(2)}) copy-start(bf16[1,2048,352]{1,2,0:T(8,128)(2,1)} %param.23) | copy-start | bytes 4325380
  451.7 12.5 all-to-all-start.3
  464.2 13.2 all-to-all-start.1
  468.8 402.8 %all-reduce.14.cloned.1.call-start = ((), (), s32[]{:S(2)}) async-start(), calls=%async_computation.5 | async-start | bytes 2097152
  481.2 955.0 %all-reduce.12.cloned.1.call-start = ((), (), s32[]{:S(2)}) async-start(), calls=%async_computation.4 | async-start | bytes 2097152
  992.7 81.3 %copy-start.4 = (bf16[128,1,2048]{2,1,0:T(2,128)(2,1)}, bf16[128,1,2048]{2,1,0:T(2,128)(2,1)S(1)}, u32[]{:S(2)}) copy-start(bf16[128,1,2048]{2,1,0:T(2,128)(2,1)S(1)} %all_gather.27) | copy-start | bytes 1572868
  1072.6 1.3 copy-start.2
  1073.9 4.1 copy-start.3
Sparse Core Ops, SparseCore 0:
  481.3 390.2 all-reduce.13
  1081.8 354.3 all-reduce.11
where the time goes:
time: 1480 us
  waiting for transfers between devices  763 us (52%)
  blocking collectives  570 us (39%)
  local copies, waits for them, and re-layouts  67.3 us (5%)
  matrix products  35 us (2%)
  starting transfers between devices  16.4 us (1%)
  between operations  15.1 us (1%)
    unnamed x4, waiting for transfers between devices  743 us
    all_gather x2, blocking collectives, section(): block_rows = lax.all_gather(hidden_normed, 'req', axis=0, tiled=True)  167 us
    all_gather x1, blocking collectives, shards(): lax.all_gather(normed[:, 0:1], 'req', axis=0, tiled=True)  88.1 us
    all_gather x1, blocking collectives, shards(): second_rows = lax.all_gather(normed[:, 1:2], 'req', axis=0, tiled=True)  82.6 us
    all_gather x1, blocking collectives, shards(): lax.all_gather(route_gates, 'req', axis=0, tiled=True)  76.8 us
    all_gather x1, blocking collectives, shards(): lax.all_gather(route_ids, 'req', axis=0, tiled=True)  75 us
    psum x2, blocking collectives, combine(): return lax.psum(partial_value, 'rep').astype(jnp.float32)  64.1 us
  transfers between devices with their start and end apart: 6, of which 5 were waited for; matrix products, arithmetic and copies ran while one was open for 5% of the time, Pallas kernels for 0%

commit v1 on v0

--- a/solution.py
+++ b/solution.py
@@ -203,7 +203,10 @@
     early = section(
         (0,), first_rows, slot_map, all_ids, all_gates, pair_kv(first_fresh, first_fresh)
     )
-    second_rows = lax.all_gather(normed[:, 1:2], "req", axis=0, tiled=True)
+    wrap_indices = lambda t0: jnp.concatenate(
+        lax.all_to_all(jnp.stack([t0 for _ in range(lax.axis_size("req"))]), "req", 0, 0), axis=0
+    )
+    second_rows = wrap_indices(normed[:, 1:2])
     second_fresh = fresh_kv(jnp.take(second_rows[:, 0], new_slot, axis=0))
     later = section(
         (1,), second_rows, slot_map, all_ids, all_gates, pair_kv(first_fresh, second_fresh)

time: 1480 us -> 1390 us (0.939)
  blocking collectives: 570 us -> 488 us
  waiting for transfers between devices: 763 us -> 744 us
    all_gather x1 -> x0, blocking collectives: 82.6 us -> none  [shards(): second_rows = lax.all_gather(normed[:, 1:2], 'req', axis=0, tiled=True)]
  transfers between devices with their start and end apart: 6 -> 7, of which waited for: 5 -> 5; matrix products, arithmetic and copies ran while one was open for 5% -> 6% of each run, Pallas kernels for 0% -> 0%
where the time goes in v1:
time: 1390 us
  waiting for transfers between devices  744 us (54%)
  blocking collectives  488 us (35%)
  local copies, waits for them, and re-layouts  68.5 us (5%)
  matrix products  37.1 us (3%)
  starting transfers between devices  29 us (2%)
  between operations  15.1 us (1%)
    unnamed x4, waiting for transfers between devices  730 us
    all_gather x2, blocking collectives, section(): block_rows = lax.all_gather(hidden_normed, 'req', axis=0, tiled=True)  167 us
    all_gather x1, blocking collectives, shards(): lax.all_gather(normed[:, 0:1], 'req', axis=0, tiled=True)  88.1 us
    all_gather x1, blocking collectives, shards(): lax.all_gather(route_gates, 'req', axis=0, tiled=True)  76.8 us
    all_gather x1, blocking collectives, shards(): lax.all_gather(route_ids, 'req', axis=0, tiled=True)  75 us
    psum x2, blocking collectives, combine(): return lax.psum(partial_value, 'rep').astype(jnp.float32)  64.1 us
  transfers between devices with their start and end apart: 7, of which 5 were waited for; matrix products, arithmetic and copies ran while one was open for 6% of the time, Pallas kernels for 0%

profile of v1, /device:TPU:1, one launch (start us, length us, event | category | flops | bytes accessed | tf_op | source)
XLA Modules:
  0.0 1390.4 jit_solution(17143646481162760606)
XLA Ops:
  6.5 1.0 multiply_reduce_fusion
  7.5 0.8 fusion.154
  8.3 0.8 multiply_convert_fusion
  9.2 88.1 %all_gather.18 = bf16[128,1,2048]{2,1,0:T(2,128)(2,1)S(1)} all-gather(bf16[4,1,2048]{2,1,0:T(2,128)(2,1)S(1)} %copy.214), channel_id=1, replica_groups=mesh['req'=32,'rep'=4] {'req'}, dimensions={0}, use_global_device_ids=true | all-gather | bytes 540672 | tf_op jit(solution)/shard_map/all_gather | solution.py:198
  97.3 2.1 convolution_convert_fusion.3
  99.4 3.9 all-to-all-start
  103.3 0.7 compare_and_fusion.2
  104.0 0.7 compare_select_fusion.3
  104.6 1.4 fusion.155
  106.7 0.9 dynamic-update-slice
  107.6 16.5 %all-reduce = s32[128]{0:T(128)S(1)} all-reduce(s32[128]{0:T(128)S(1)} %dynamic-update-slice), channel_id=1, replica_groups=mesh['req'=32,'rep'=4] {'req'}, use_global_device_ids=true, to_apply=%add | all-reduce | flops 128 | bytes 1024
  124.1 1.0 scatter_custom_fusion
  125.7 0.7 slice_bitcast_fusion.1
  126.4 0.8 copy.230
  127.2 0.7 compare_select_fusion
  128.0 0.7 iota_compare_fusion
  128.7 0.8 copy.232
  129.5 2.8 fusion.46
  132.3 76.8 %all_gather.20 = bf16[128,2,2,2]{3,2,1,0:T(2,128)(2,1)S(1)} all-gather(bf16[4,2,2,2]{3,2,1,0:T(2,128)(2,1)S(1)} %copy.232), channel_id=1, replica_groups=mesh['req'=32,'rep'=4] {'req'}, dimensions={0}, use_global_device_ids=true | all-gather | bytes 2112 | tf_op jit(solution)/shard_map/all_gather | solution.py:200
  209.1 0.8 fusion.153
  209.9 75.0 %all_gather.19 = s32[128,2,2,2]{3,2,1,0:T(2,128)S(1)} all-gather(s32[4,2,2,2]{3,2,1,0:T(2,128)S(1)} %copy.230), channel_id=1, replica_groups=mesh['req'=32,'rep'=4] {'req'}, dimensions={0}, use_global_device_ids=true | all-gather | bytes 4224 | tf_op jit(solution)/shard_map/all_gather | solution.py:199
  285.0 0.8 fusion.152
  285.8 25.4 %gather_fusion = bf16[256,16,2,512]{3,2,1,0:T(2,128)(2,1)} fusion(bf16[256,16,2,512]{3,2,1,0:T(2,128)(2,1)} %param.26, s32[1024]{0:T(1024)S(1)} %pad_clamp_fusion.3), kind=kCustom, calls=%fused_computation.2 | custom fusion | bytes 16778240 | tf_op jit(solution)/shard_map/gather | solution.py:88
  311.2 14.0 %reshape.559 = bf16[4,1024,2,4,128]{4,3,2,1,0:T(4,128)(2,1)} reshape(bf16[256,16,2,512]{3,2,1,0:T(2,128)(2,1)} %gather_fusion) | data formatting | bytes 16777216 | tf_op jit(solution)/shard_map/reshape | solution.py:88
  325.2 8.1 fusion.151
  333.9 0.7 select_reduce_fusion.1
  334.7 1.0 stack.12
  335.8 4.5 all-to-all-start.2
  340.8 3.5 fusion.156
  345.4 3.0 fusion.1
  348.7 0.6 copy.229
  349.4 2.0 all-to-all-done.2
  352.3 0.7 gather_fusion.3
  353.0 0.7 broadcast_select_fusion
  353.7 7.4 all-to-all-start.3
  361.2 2.9 fusion.49
  364.1 5.5 all-to-all-done.3
  369.6 3.9 all-to-all-start.1
  373.7 3.5 fusion.157
  378.2 3.6 fusion
  381.9 0.7 copy.250
  382.6 1.6 fusion.43
  384.2 0.8 copy.251
  386.2 9.2 all-to-all-start.4
  395.5 1.8 fusion.15
  397.4 6.7 all-to-all-done.4
  404.1 1.3 gather_fusion.4
  405.4 1.9 fusion.13
  408.0 1.0 select_reduce_fusion
  409.1 375.6 %all-reduce.14.cloned.1.call-done = (bf16[128,1,2048]{2,0,1:T(8,128)(2,1)}, bf16[128,1,2048]{2,0,1:T(8,128)(2,1)}) async-done(((bf16[128,1,2048]{2,0,1:T(8,128)(2,1)}, bf16[128,1,2048]{2,0,1:T(8,128)(2,1)}), (bf16[128,1,2048]{2,0,1:T(8,128)(2,1)}, bf16[128,1,2048]{2,0,1:T(8,128)(2,1)})) %all-reduce.14.cloned.1.call-update) | async-done | bytes 1048592
  784.6 0.8 constant_dynamic-slice_fusion.3
  785.4 0.8 constant_dynamic-slice_fusion.1
  786.2 32.1 %all-reduce.8 = (bf16[4,1,2048]{2,0,1:T(4,128)(2,1)S(1)}, bf16[4,1,2048]{2,0,1:T(4,128)(2,1)S(1)}) all-reduce(bf16[4,1,2048]{2,0,1:T(4,128)(2,1)S(1)} %constant_dynamic-slice_fusion.3, bf16[4,1,2048]{2,0,1:T(4,128)(2,1)S(1)} %constant_dynamic-slice_fusion.1), channel_id=1, replica_groups=mesh['req'=32,'rep'=4] {'rep'}, use_global_device_ids=true, to_apply=%region_7.8 | all-reduce | flops 16384 | bytes 65536 | tf_op jit(solution)/shard_map/psum | solution.py:59
  818.6 87.1 %all_gather.23 = bf16[128,1,2048]{2,1,0:T(2,128)(2,1)S(1)} all-gather(bf16[4,1,2048]{2,1,0:T(2,128)(2,1)S(1)} %copy.254), channel_id=1, replica_groups=mesh['req'=32,'rep'=4] {'req'}, dimensions={0}, use_global_device_ids=true | all-gather | bytes 540672 | tf_op jit(solution)/shard_map/all_gather | solution.py:180
  905.7 79.9 %all_gather.21 = bf16[128,1,2048]{2,1,0:T(2,128)(2,1)S(1)} all-gather(bf16[4,1,2048]{2,1,0:T(2,128)(2,1)S(1)} %copy.234), channel_id=1, replica_groups=mesh['req'=32,'rep'=4] {'req'}, dimensions={0}, use_global_device_ids=true | all-gather | bytes 540672 | tf_op jit(solution)/shard_map/all_gather | solution.py:180
  985.7 0.6 fusion.22
  986.3 0.6 fusion.24
  987.0 4.1 fusion.12
  991.1 3.7 fusion.14
  994.8 354.5 %all-reduce.12.cloned.1.call-done = (bf16[128,1,2048]{2,0,1:T(8,128)(2,1)}, bf16[128,1,2048]{2,0,1:T(8,128)(2,1)}) async-done(((bf16[128,1,2048]{2,0,1:T(8,128)(2,1)}, bf16[128,1,2048]{2,0,1:T(8,128)(2,1)}), (bf16[128,1,2048]{2,0,1:T(8,128)(2,1)}, bf16[128,1,2048]{2,0,1:T(8,128)(2,1)})) %all-reduce.12.cloned.1.call-update) | async-done | bytes 1048592
  1349.3 0.8 constant_dynamic-slice_fusion
  1350.0 0.8 constant_dynamic-slice_fusion.2
  1350.8 32.1 %all-reduce.7 = (bf16[4,1,2048]{2,0,1:T(4,128)(2,1)S(1)}, bf16[4,1,2048]{2,0,1:T(4,128)(2,1)S(1)}) all-reduce(bf16[4,1,2048]{2,0,1:T(4,128)(2,1)S(1)} %constant_dynamic-slice_fusion, bf16[4,1,2048]{2,0,1:T(4,128)(2,1)S(1)} %constant_dynamic-slice_fusion.2), channel_id=1, replica_groups=mesh['req'=32,'rep'=4] {'rep'}, use_global_device_ids=true, to_apply=%region_23.25 | all-reduce | flops 16384 | bytes 65536 | tf_op jit(solution)/shard_map/psum | solution.py:59
  1383.0 0.6 copy.257
  (93 shorter events, 7.4 us)
Async XLA Ops:
  6.5 980.5 %copy-start = (bf16[1,352,2048]{2,1,0:T(8,128)(2,1)S(1)}, bf16[1,352,2048]{2,1,0:T(8,128)(2,1)}, u32[]{:S(2)}) copy-start(bf16[1,352,2048]{2,1,0:T(8,128)(2,1)} %param.25) | copy-start | bytes 4325380
  99.4 235.3 %all-to-all-start = ((bf16[32,4,1,128]{3,1,2,0:T(4,128)(2,1)}), bf16[32,4,1,128]{3,1,2,0:T(4,128)(2,1)S(1)}, u32[]{:S(2)}, u32[]{:S(2)}) async-start(bf16[32,4,1,128]{3,1,2,0:T(4,128)(2,1)} %bitcast.8), calls=%async_computation | async-start | bytes 65536 | tf_op jit(solution)/shard_map/all_to_all | solution.py:127
  333.9 39.6 %copy-start.12 = (s32[4,2]{1,0:T(4,128)}, s32[4,2]{1,0:T(4,128)S(1)}, u32[]{:S(2)}) copy-start(s32[4,2]{1,0:T(4,128)S(1)} %broadcast_select_fusion.1) | copy-start | bytes 100
  333.9 10.5 copy-start.11
  334.7 42.4 %copy-start.9 = (bf16[4,1,2,4,128]{4,1,3,0,2:T(2,128)(2,1)}, bf16[4,1,2,4,128]{4,1,3,0,2:T(2,128)(2,1)S(1)}, u32[]{:S(2)}) copy-start(bf16[4,1,2,4,128]{4,1,3,0,2:T(2,128)(2,1)S(1)} %stack.16) | copy-start | bytes 24580
  335.8 15.5 %all-to-all-start.2 = ((bf16[32,4,1,2048]{3,1,2,0:T(4,128)(2,1)}), bf16[32,4,1,2048]{3,1,2,0:T(4,128)(2,1)S(1)}, u32[]{:S(2)}, u32[]{:S(2)}) async-start(bf16[32,4,1,2048]{3,1,2,0:T(4,128)(2,1)} %stack.12), calls=%async_computation.2 | async-start | bytes 1048576 | tf_op jit(solution)/shard_map/all_to_all | solution.py:207
  345.4 6.6 copy-start.6
  353.7 15.9 %all-to-all-start.3 = ((bf16[32,4,1,128]{3,1,2,0:T(4,128)(2,1)}), bf16[32,4,1,128]{3,1,2,0:T(4,128)(2,1)S(1)}, u32[]{:S(2)}, u32[]{:S(2)}) async-start(bf16[32,4,1,128]{3,1,2,0:T(4,128)(2,1)} %bitcast.40), calls=%async_computation.3 | async-start | bytes 65536 | tf_op jit(solution)/shard_map/all_to_all | solution.py:127
  364.1 14.0 %copy-start.10 = (bf16[4,1,2,4,128]{4,1,3,0,2:T(2,128)(2,1)}, bf16[4,1,2,4,128]{4,1,3,0,2:T(2,128)(2,1)S(1)}, u32[]{:S(2)}) copy-start(bf16[4,1,2,4,128]{4,1,3,0,2:T(2,128)(2,1)S(1)} %stack.15) | copy-start | bytes 24580
  369.6 16.0 %all-to-all-start.1 = ((bf16[32,4,1,128]{3,1,2,0:T(4,128)(2,1)}), bf16[32,4,1,128]{3,1,2,0:T(4,128)(2,1)S(1)}, u32[]{:S(2)}, u32[]{:S(2)}) async-start(bf16[32,4,1,128]{3,1,2,0:T(4,128)(2,1)} %copy.229), calls=%async_computation.1 | async-start | bytes 65536 | tf_op jit(solution)/shard_map/all_to_all | solution.py:150
  378.2 17.3 %copy-start.5 = (bf16[1,128,2048]{2,1,0:T(8,128)(2,1)S(1)}, bf16[1,128,2048]{2,1,0:T(8,128)(2,1)}, u32[]{:S(2)}) copy-start(bf16[1,128,2048]{2,1,0:T(8,128)(2,1)} %param.22) | copy-start | bytes 1572868
  378.2 30.8 %copy-start.7 = (bf16[4,2,2048]{2,1,0:T(2,128)(2,1)S(1)}, bf16[4,2,2048]{2,1,0:T(2,128)(2,1)}, u32[]{:S(2)}) copy-start(bf16[4,2,2048]{2,1,0:T(2,128)(2,1)} %param.18) | copy-start | bytes 98308
  381.9 603.8 %copy-start.1 = (bf16[1,2048,352]{1,2,0:T(8,128)(2,1)S(1)}, bf16[1,2048,352]{1,2,0:T(8,128)(2,1)}, u32[]{:S(2)}) copy-start(bf16[1,2048,352]{1,2,0:T(8,128)(2,1)} %param.23) | copy-start | bytes 4325380
  385.6 0.6 copy-start.8
  386.2 17.9 %all-to-all-start.4 = ((bf16[32,4,1,128]{3,1,2,0:T(4,128)(2,1)}), bf16[32,4,1,128]{3,1,2,0:T(4,128)(2,1)S(1)}, u32[]{:S(2)}, u32[]{:S(2)}) async-start(bf16[32,4,1,128]{3,1,2,0:T(4,128)(2,1)} %copy.252), calls=%async_computation.4 | async-start | bytes 65536 | tf_op jit(solution)/shard_map/all_to_all | solution.py:150
  395.5 389.2 %all-reduce.14.cloned.1.call-start = ((), (), s32[]{:S(2)}) async-start(), calls=%async_computation.6 | async-start | bytes 2097152
  407.3 941.9 %all-reduce.12.cloned.1.call-start = ((), (), s32[]{:S(2)}) async-start(), calls=%async_computation.5 | async-start | bytes 2097152
  905.7 81.2 %copy-start.4 = (bf16[128,1,2048]{2,1,0:T(2,128)(2,1)}, bf16[128,1,2048]{2,1,0:T(2,128)(2,1)S(1)}, u32[]{:S(2)}) copy-start(bf16[128,1,2048]{2,1,0:T(2,128)(2,1)S(1)} %all_gather.23) | copy-start | bytes 1572868
  985.7 1.3 copy-start.2
  987.0 4.1 copy-start.3
Sparse Core Ops, SparseCore 0:
  407.5 377.1 all-reduce.13
  994.9 354.3 all-reduce.11
